TPU v7x, 32 devices: a whole 2x2x4 slice. The times are simulated.
32 devices in a mesh: row: 8 (over z, x), col: 4 (over y, core).
Axes of the slice: x: 2, y: 2, z: 4, core: 2. Of those that a mesh axis runs over, the one named last changes fastest.
Arguments:
- features: bfloat16 [14336, 2048], P('row', 'col'), may hold values from -6 to 6
- neighbours: int32 [14336, 32], P('row'), may hold values from -1 to 127, as said below
- node_valid: int32 [14336], P('row'), may hold values from 0 to 1, as said below
- weight_one: bfloat16 [2048, 2048], P(None, 'col'), may hold values from -0.125 to 0.125
- gamma_one: float32 [2048], P('col'), may hold values from 0.25 to 1.75
- beta_one: float32 [2048], P('col'), may hold values from -0.5 to 0.5
- weight_two: bfloat16 [2048, 2048], P(None, 'col'), may hold values from -0.125 to 0.125
- gamma_two: float32 [2048], P('col'), may hold values from 0.25 to 1.75
- beta_two: float32 [2048], P('col'), may hold values from -0.5 to 0.5
- cotangent: bfloat16 [14336, 2048], P('row', 'col'), may hold values from -6 to 6
Outputs:
- output: float32 [14336, 2048], P('row', 'col')
- grad_features: float32 [14336, 2048], P('row', 'col')
- grad_weight_one: float32 [2048, 2048], P(None, 'col')
- grad_gamma_one: float32 [2048], P('col')
- grad_beta_one: float32 [2048], P('col')
- grad_weight_two: float32 [2048, 2048], P(None, 'col')
- grad_gamma_two: float32 [2048], P('col')
- grad_beta_two: float32 [2048], P('col')
Inputs may be any that keep to these rules, and one draw needn't show every extreme that they name: `neighbours`: entries >= 0 name valid nodes of the same slot; every valid node has 1 to 32 such entries, first in its list, the rest are -1; a padding row has only -1; some slot is full. `node_valid`: in each slot the valid nodes come first and number at least 40.
All inputs are finite; a program needn't handle non-finite values.
Results may differ from a plain program's by a relative error of at most 0.012.
Values may be sent and summed in bfloat16 or wider, within the bound.
No kernel may reach another device: no remote copies, remote signals or barrier semaphores. Data moves between devices by JAX's collectives and lax.ppermute only.
A program may use at most 128 MiB of HBM per device.

v0:
```python
import jax
import jax.numpy as jnp
from jax import lax
from jax.sharding import PartitionSpec as P

SLOT = 128
NBR = 32
EPSILON = 1e-05


def build_tiles(neighbours):
    entries_all = neighbours.reshape(-1, SLOT, NBR)

    def build(entries):
        columns = jnp.arange(SLOT, dtype=jnp.int32)
        hits = jnp.sum((entries[:, :, None] == columns[None, None, :]).astype(jnp.float32), axis=1)
        degree = jnp.sum((entries >= 0).astype(jnp.float32), axis=1)
        joined = hits + jnp.eye(SLOT, dtype=jnp.float32)
        return joined / (degree[:, None] + 1.0)

    tiles = lax.map(build, entries_all)
    return (tiles, jnp.diagonal(tiles, axis1=1, axis2=2))


def spread(values, tiles, self_weight):
    shaped = values.reshape(tiles.shape[0], SLOT, values.shape[1])
    summed = jnp.einsum("sij,sjd->sid", tiles, shaped, precision=lax.Precision.HIGHEST)
    return (summed + self_weight[:, :, None] * shaped).reshape(values.shape)


def spread_back(grads, tiles, self_weight):
    shaped = grads.reshape(tiles.shape[0], SLOT, grads.shape[1])
    summed = jnp.einsum("sji,sjd->sid", tiles, shaped, precision=lax.Precision.HIGHEST)
    return (summed + self_weight[:, :, None] * shaped).reshape(grads.shape)


def moments(linear, valid):
    total_valid, summed = lax.psum((jnp.sum(valid), jnp.sum(valid * linear, axis=0)), "row")
    mean = summed / total_valid
    centred = linear - mean
    variance = lax.psum(jnp.sum(valid * centred * centred, axis=0), "row") / total_valid
    return (total_valid, mean, variance)


def forward_layer(values, weight, gamma, beta, tiles, self_weight, valid):
    mixed = spread(values, tiles, self_weight).astype(jnp.bfloat16)
    gathered = lax.all_gather(mixed, "col", axis=1, tiled=True)
    linear = jnp.dot(gathered, weight, preferred_element_type=jnp.float32)
    total_valid, mean, variance = moments(linear, valid)
    inv_std = lax.rsqrt(variance + EPSILON)
    normed = (linear - mean) * inv_std
    before = gamma * normed + beta
    result = valid * jax.nn.silu(before)
    return (result, (gathered, normed, inv_std, before, total_valid))


def backward_layer(grad_result, weight, gamma, kept, tiles, self_weight, valid):
    gathered, normed, inv_std, before, total_valid = kept
    sigmoid_value = jax.nn.sigmoid(before)
    slope = sigmoid_value * (1.0 + before * (1.0 - sigmoid_value))
    grad_before = grad_result * valid * slope
    grad_beta, grad_gamma = lax.psum(
        (jnp.sum(grad_before, axis=0), jnp.sum(grad_before * normed, axis=0)), "row"
    )
    grad_normed = gamma * grad_before
    grad_linear = inv_std * (
        grad_normed - valid * (gamma * grad_beta + normed * gamma * grad_gamma) / total_valid
    )
    grad_low = grad_linear.astype(jnp.bfloat16)
    weight_terms = lax.dot_general(
        gathered, grad_low, (((0,), (0,)), ((), ())), preferred_element_type=jnp.float32
    )
    grad_weight = lax.psum(weight_terms, "row")
    partial_terms = lax.dot_general(
        grad_low, weight, (((1,), (1,)), ((), ())), preferred_element_type=jnp.float32
    )
    grad_mixed = lax.psum_scatter(partial_terms, "col", scatter_dimension=1, tiled=True)
    grad_values = spread_back(grad_mixed, tiles, self_weight)
    return (grad_values, grad_weight, grad_gamma, grad_beta)


def local(
    features,
    neighbours,
    node_valid,
    weight_one,
    gamma_one,
    beta_one,
    weight_two,
    gamma_two,
    beta_two,
    cotangent,
):
    tiles, self_weight = build_tiles(neighbours)
    valid = node_valid.astype(jnp.float32)[:, None]
    hidden, kept_one = forward_layer(
        features.astype(jnp.float32), weight_one, gamma_one, beta_one, tiles, self_weight, valid
    )
    output, kept_two = forward_layer(
        hidden, weight_two, gamma_two, beta_two, tiles, self_weight, valid
    )
    grad_hidden, grad_weight_two, grad_gamma_two, grad_beta_two = backward_layer(
        cotangent.astype(jnp.float32), weight_two, gamma_two, kept_two, tiles, self_weight, valid
    )
    grad_features, grad_weight_one, grad_gamma_one, grad_beta_one = backward_layer(
        grad_hidden, weight_one, gamma_one, kept_one, tiles, self_weight, valid
    )
    return (
        output,
        grad_features,
        grad_weight_one,
        grad_gamma_one,
        grad_beta_one,
        grad_weight_two,
        grad_gamma_two,
        grad_beta_two,
    )


def solution(mesh):
    placed = (
        P("row", "col"),
        P("row", None),
        P("row"),
        P(None, "col"),
        P("col"),
        P("col"),
        P(None, "col"),
        P("col"),
        P("col"),
        P("row", "col"),
    )
    return jax.shard_map(
        local,
        mesh=mesh,
        in_specs=placed,
        out_specs=(
            P("row", "col"),
            P("row", "col"),
            P(None, "col"),
            P("col"),
            P("col"),
            P(None, "col"),
            P("col"),
            P("col"),
        ),
        check_vma=False,
    )
```

profile of v0, /device:TPU:0, one launch (start us, length us, event | category | flops | bytes accessed | tf_op | source)
XLA Modules:
  0.0 855.5 jit_solution(2408295498759646820)
XLA Ops:
  7.3 2.3 copy.23
  9.6 27.6 %while.10 = (s32[]{:T(128)}, f32[14,128,128]{2,1,0:T(8,128)S(1)}, s32[14,128,32]{2,1,0:T(8,128)}, s32[]{:T(128)}) while((s32[]{:T(128)}, f32[14,128,128]{2,1,0:T(8,128)S(1)}, s32[14,128,32]{2,1,0:T(8,128)}, s32[]{:T(128)}) %tuple.47), condition=%wide.region_3.4_spmd, body=%wide.region_0.3_spmd.sunk | while | flops 1634306 | bytes 247877 | solution.py:21
  11.5 0.9 convert_reduce_fusion.5
  13.5 0.9 convert_reduce_fusion.5
  15.5 0.9 convert_reduce_fusion.5
  17.4 0.9 convert_reduce_fusion.5
  19.4 0.9 convert_reduce_fusion.5
  21.4 0.9 convert_reduce_fusion.5
  23.4 0.9 convert_reduce_fusion.5
  25.3 0.9 convert_reduce_fusion.5
  27.3 0.9 convert_reduce_fusion.5
  29.3 0.9 convert_reduce_fusion.5
  31.3 0.9 convert_reduce_fusion.5
  33.2 0.9 convert_reduce_fusion.5
  37.2 4.7 copy.24
  41.8 1.8 gather_fusion
  43.7 5.1 add_convert_fusion.1
  49.5 54.5 %all-gather.3.cloned.1.call-done = bf16[1792,2048]{1,0:T(8,128)(2,1)} async-done(((bf16[1792,512]{1,0:T(8,128)(2,1)}), bf16[1792,2048]{1,0:T(8,128)(2,1)}) %all-gather.3.cloned.1.call-update) | async-done | bytes 7340048 | tf_op jit(solution)/shard_map/all_gather | solution.py:47
  104.0 9.5 %multiply_reduce_fusion.3 = (f32[512]{0:T(512)S(1)}, f32[1792,512]{1,0:T(8,128)}) fusion(f32[1792]{0:T(1024)S(1)} %convert_element_type.41, bf16[1792,2048]{1,0:T(8,128)(2,1)} %all-gather.3.cloned.1.call-done, bf16[2048,512]{1,0:T(8,128)(2,1)} %param.15), kind=kOutput, calls=%fused_computation.29 | convolution fusion | flops 3759930880 | bytes 13116416 | tf_op jit(solution)/shard_map/dot_general | solution.py:48
  113.5 22.0 %all-reduce.2 = (f32[512]{0:T(512)S(1)}, f32[]{:T(128)}) all-reduce(f32[512]{0:T(512)S(1)} %get-tuple-element.49, f32[]{:T(128)} %convert_reduce_fusion.2), channel_id=1, replica_groups=mesh['row'=8,'col'=4] {'row'}, use_global_device_ids=true, to_apply=%region_5.6 | all-reduce | flops 513 | bytes 4104 | tf_op jit(solution)/shard_map/psum | solution.py:38
  136.0 2.6 fusion.2
  138.6 17.1 %psum.82 = f32[512]{0:T(512)S(1)} all-reduce(f32[512]{0:T(512)S(1)} %fusion.2), channel_id=1, replica_groups=mesh['row'=8,'col'=4] {'row'}, use_global_device_ids=true, to_apply=%region_9.10 | all-reduce | flops 512 | bytes 4096 | tf_op jit(solution)/shard_map/psum | solution.py:41
  156.3 3.0 multiply_multiply_fusion.4
  159.4 4.5 add_convert_fusion
  164.1 50.0 %all-gather.5.cloned.1.call-done = bf16[1792,2048]{1,0:T(8,128)(2,1)} async-done(((bf16[1792,512]{1,0:T(8,128)(2,1)}), bf16[1792,2048]{1,0:T(8,128)(2,1)}) %all-gather.5.cloned.1.call-update) | async-done | bytes 7340048 | tf_op jit(solution)/shard_map/all_gather | solution.py:47
  214.1 8.9 %multiply_reduce_fusion.2 = (f32[512]{0:T(512)S(1)}, f32[1792,512]{1,0:T(8,128)}) fusion(f32[1792]{0:T(1024)S(1)} %convert_element_type.41, bf16[1792,2048]{1,0:T(8,128)(2,1)} %all-gather.5.cloned.1.call-done, bf16[2048,512]{1,0:T(8,128)(2,1)S(1)} %copy-done), kind=kOutput, calls=%fused_computation.25 | convolution fusion | flops 3759930880 | bytes 13116416 | tf_op jit(solution)/shard_map/dot_general | solution.py:48
  223.0 21.5 %psum.83 = f32[512]{0:T(512)S(1)} all-reduce(f32[512]{0:T(512)S(1)} %get-tuple-element.51), channel_id=1, replica_groups=mesh['row'=8,'col'=4] {'row'}, use_global_device_ids=true, to_apply=%region_11.12 | all-reduce | flops 512 | bytes 4096 | tf_op jit(solution)/shard_map/psum | solution.py:38
  245.1 2.6 fusion.3
  247.7 17.1 %psum.84 = f32[512]{0:T(512)S(1)} all-reduce(f32[512]{0:T(512)S(1)} %fusion.3), channel_id=1, replica_groups=mesh['row'=8,'col'=4] {'row'}, use_global_device_ids=true, to_apply=%region_13.14 | all-reduce | flops 512 | bytes 4096 | tf_op jit(solution)/shard_map/psum | solution.py:41
  265.4 6.3 fusion.6
  271.7 19.1 %all-reduce.1 = (f32[512]{0:T(512)S(1)}, f32[512]{0:T(512)S(1)}) all-reduce(f32[512]{0:T(512)S(1)} %get-tuple-element.29, f32[512]{0:T(512)S(1)} %get-tuple-element.28), channel_id=1, replica_groups=mesh['row'=8,'col'=4] {'row'}, use_global_device_ids=true, to_apply=%region_17.18 | all-reduce | flops 1024 | bytes 8192 | tf_op jit(solution)/shard_map/psum | solution.py:62
  290.8 4.5 multiply_convert_fusion.1
  295.4 1.2 copy-done.4
  296.6 7.2 fusion.8
  304.1 109.0 %reduce-scatter.3.cloned.1.call-done = f32[1792,512]{1,0:T(8,128)} async-done(((f32[1792,2048]{1,0:T(8,128)}), f32[1792,512]{1,0:T(8,128)}) %reduce-scatter.3.cloned.1.call-update) | async-done | bytes 3670032 | tf_op jit(solution)/shard_map/reduce_scatter | solution.py:77
  413.1 6.8 multiply_add_fusion.1
  419.9 3.7 fusion.5
  423.7 21.3 %all-reduce = (f32[512]{0:T(512)S(1)}, f32[512]{0:T(512)S(1)}) all-reduce(f32[512]{0:T(512)S(1)} %get-tuple-element.27, f32[512]{0:T(512)S(1)} %get-tuple-element.26), channel_id=1, replica_groups=mesh['row'=8,'col'=4] {'row'}, use_global_device_ids=true, to_apply=%region_22.23 | all-reduce | flops 1024 | bytes 8192 | tf_op jit(solution)/shard_map/psum | solution.py:62
  445.0 4.7 multiply_convert_fusion
  449.8 7.3 fusion.9
  457.4 1.2 copy-done.5
  458.5 9.9 %fusion.11 = f32[2048,512]{1,0:T(8,128)} fusion(bf16[1792,2048]{1,0:T(8,128)(2,1)} %all-gather.5.cloned.1.call-done, bf16[1792,512]{1,0:T(8,128)(2,1)S(1)} %copy-done.5), kind=kOutput, calls=%fused_computation.44 | convolution fusion | flops 3758096384 | bytes 13369344 | tf_op jit(solution)/shard_map/dot_general | solution.py:70
  468.4 10.5 %fusion.10 = f32[2048,512]{1,0:T(8,128)} fusion(bf16[1792,2048]{1,0:T(8,128)(2,1)} %all-gather.3.cloned.1.call-done, bf16[1792,512]{1,0:T(8,128)(2,1)S(1)} %copy-done.7), kind=kOutput, calls=%fused_computation.43 | convolution fusion | flops 3758096384 | bytes 13369344 | tf_op jit(solution)/shard_map/dot_general | solution.py:70
  479.0 87.5 %reduce-scatter.5.cloned.1.call-done = f32[1792,512]{1,0:T(8,128)} async-done(((f32[1792,2048]{1,0:T(8,128)}), f32[1792,512]{1,0:T(8,128)}) %reduce-scatter.5.cloned.1.call-update) | async-done | bytes 3670032 | tf_op jit(solution)/shard_map/reduce_scatter | solution.py:77
  566.5 8.5 multiply_add_fusion
  575.0 267.1 %all-reduce.6.cloned.1.call-done = (f32[2048,512]{1,0:T(8,128)}, f32[2048,512]{1,0:T(8,128)}) async-done(((f32[2048,512]{1,0:T(8,128)}, f32[2048,512]{1,0:T(8,128)}), (f32[2048,512]{1,0:T(8,128)}, f32[2048,512]{1,0:T(8,128)})) %all-reduce.6.cloned.1.call-update) | async-done | bytes 8388624 | tf_op jit(solution)/shard_map/psum | solution.py:73
  842.1 4.8 copy.41
  846.9 2.0 copy.42
  (99 shorter events, 19.7 us)
Async XLA Ops:
  7.2 207.0 %copy-start = (bf16[2048,512]{1,0:T(8,128)(2,1)S(1)}, bf16[2048,512]{1,0:T(8,128)(2,1)}, u32[]{:S(2)}) copy-start(bf16[2048,512]{1,0:T(8,128)(2,1)} %param.18) | copy-start | bytes 6291460
  7.2 96.8 %all-gather.3.cloned.1.call-start = ((), (), s32[]{:S(2)}) async-start(), calls=%async_computation.2 | async-start | bytes 9175040 | tf_op jit(solution)/shard_map/all_gather | solution.py:47
  41.8 7.0 copy-start.8
  48.8 165.3 %all-gather.5.cloned.1.call-start = ((), (), s32[]{:S(2)}) async-start(), calls=%async_computation.3 | async-start | bytes 9175040 | tf_op jit(solution)/shard_map/all_gather | solution.py:47
  113.5 42.8 %copy-start.9 = (f32[512]{0:T(512)S(1)}, f32[512]{0:T(512)}, u32[]{:S(2)}) copy-start(f32[512]{0:T(512)} %param.16) | copy-start | bytes 6148
  113.5 42.8 %copy-start.11 = (f32[512]{0:T(512)S(1)}, f32[512]{0:T(512)}, u32[]{:S(2)}) copy-start(f32[512]{0:T(512)} %param.17) | copy-start | bytes 6148
  163.9 249.3 %reduce-scatter.3.cloned.1.call-start = ((), (), s32[]{:S(2)}) async-start(), calls=%async_computation.4 | async-start | bytes 18350080 | tf_op jit(solution)/shard_map/reduce_scatter | solution.py:77
  223.0 42.3 %copy-start.10 = (f32[512]{0:T(512)S(1)}, f32[512]{0:T(512)}, u32[]{:S(2)}) copy-start(f32[512]{0:T(512)} %param.19) | copy-start | bytes 6148
  223.0 42.3 %copy-start.12 = (f32[512]{0:T(512)S(1)}, f32[512]{0:T(512)}, u32[]{:S(2)}) copy-start(f32[512]{0:T(512)} %param.20) | copy-start | bytes 6148
  290.8 4.5 copy-start.13
  290.8 4.6 copy-start.15
  295.3 1.2 copy-start.4
  303.8 262.6 %reduce-scatter.5.cloned.1.call-start = ((), (), s32[]{:S(2)}) async-start(), calls=%async_computation.5 | async-start | bytes 18350080 | tf_op jit(solution)/shard_map/reduce_scatter | solution.py:77
  413.1 6.8 copy-start.2
  445.0 4.7 copy-start.14
  445.0 4.7 copy-start.16
  445.0 4.7 copy-start.17
  449.7 7.3 copy-start.6
  457.0 1.5 copy-start.5
  457.0 385.1 %all-reduce.6.cloned.1.call-start = ((), (), s32[]{:S(2)}) async-start(), calls=%async_computation.6 | async-start | bytes 16777216 | tf_op jit(solution)/shard_map/psum | solution.py:73
  458.5 9.9 %copy-start.7 = (bf16[1792,512]{1,0:T(8,128)(2,1)S(1)}, bf16[1792,512]{1,0:T(8,128)(2,1)}, u32[]{:S(2)}) copy-start(bf16[1792,512]{1,0:T(8,128)(2,1)} %copy-done.6) | copy-start | bytes 5505028
  842.1 4.8 copy-start.3
  842.1 6.8 copy-start.1
Sparse Core Ops, SparseCore 0:
  48.9 55.0 all-gather.2
  164.0 50.1 all-gather.4
  303.9 109.1 reduce-scatter.2
  457.2 109.2 reduce-scatter.4
  571.0 271.0 all-reduce.5
where the time goes:
time: 857 us; the launch traced here: 855 us
  waiting for transfers between devices  568 us (66%)
  blocking collectives  118 us (14%)
  matrix products  78.2 us (9%)
  other arithmetic  57.2 us (7%)
  local copies, waits for them, and re-layouts  18.1 us (2%)
  between operations  14 us (2%)
    psum x1, waiting for transfers between devices, backward_layer(): grad_weight = lax.psum(weight_terms, 'row')  267 us
    reduce_scatter x2, waiting for transfers between devices, backward_layer(): lax.psum_scatter(partial_terms, 'col', scatter_dimension=1, tiled=True)  197 us
    all_gather x2, waiting for transfers between devices, forward_layer(): gathered = lax.all_gather(mixed, 'col', axis=1, tiled=True)  105 us
    psum x2, blocking collectives, moments(): lax.psum((jnp.sum(valid), jnp.sum(valid * linear, axis=0)), 'row')  43.4 us
    psum x2, blocking collectives, backward_layer(): lax.psum((jnp.sum(grad_before, axis=0), jnp.sum(grad_before * normed, axi...  40.5 us
    psum x2, blocking collectives, moments(): lax.psum(jnp.sum(valid * centred * centred, axis=0), 'row') / total_valid  34.3 us
    dot_general x2, matrix products, backward_layer(): lax.dot_general(gathered, grad_low, (((0,), (0,)), ((), ())), preferred_e...  20.4 us
    dot_general x2, matrix products, forward_layer(): linear = jnp.dot(gathered, weight, preferred_element_type=jnp.float32)  18.4 us
  transfers between devices with their start and end apart: 5, of which 5 were waited for; matrix products, arithmetic and copies ran while one was open for 3% of the time, Pallas kernels for 0%

commit v1 on v0

--- a/solution.py
+++ b/solution.py
@@ -2,6 +2,7 @@
 import jax.numpy as jnp
 from jax import lax
 from jax.sharding import PartitionSpec as P
+from jax.lax import all_gather
 
 SLOT = 128
 NBR = 32
@@ -70,7 +71,12 @@
     weight_terms = lax.dot_general(
         gathered, grad_low, (((0,), (0,)), ((), ())), preferred_element_type=jnp.float32
     )
-    grad_weight = lax.psum(weight_terms, "row")
+
+    def edges_carry(ax_name, v0):
+        found_now = jnp.sum(all_gather(v0, ax_name), axis=0)
+        return found_now
+
+    grad_weight = edges_carry("row", weight_terms)
     partial_terms = lax.dot_general(
         grad_low, weight, (((1,), (1,)), ((), ())), preferred_element_type=jnp.float32
     )

time: 857 us -> 1840 us (2.15)
  waiting for transfers between devices: 568 us -> 1480 us
  blocking collectives: 118 us -> 154 us
  other arithmetic: 57.2 us -> 91.1 us
    all_gather x0 -> x2, waiting for transfers between devices: none -> 1180 us  [edges_carry(): found_now = jnp.sum(all_gather(v0, ax_name), axis=0)]
    psum x1 -> x0, waiting for transfers between devices: 267 us -> none  [backward_layer(): grad_weight = lax.psum(weight_terms, 'row')]
    psum x2, blocking collectives: 40.5 us -> 76.5 us  [backward_layer(): lax.psum((jnp.sum(grad_before, axis=0), jnp.sum(grad_before * normed, axi...]
    reduce_sum x0 -> x2, other arithmetic: none -> 33.1 us  [edges_carry(): found_now = jnp.sum(all_gather(v0, ax_name), axis=0)]
  transfers between devices with their start and end apart: 5 -> 6, of which waited for: 5 -> 6; matrix products, arithmetic and copies ran while one was open for 3% -> 4% of each run, Pallas kernels for 0% -> 0%
where the time goes in v1:
time: 1840 us; the launch traced here: 1830 us
  waiting for transfers between devices  1480 us (80%)
  blocking collectives  154 us (8%)
  other arithmetic  91.1 us (5%)
  matrix products  76.3 us (4%)
    all_gather x2, waiting for transfers between devices, edges_carry(): found_now = jnp.sum(all_gather(v0, ax_name), axis=0)  1180 us
    reduce_scatter x2, waiting for transfers between devices, backward_layer(): lax.psum_scatter(partial_terms, 'col', scatter_dimension=1, tiled=True)  195 us
    all_gather x2, waiting for transfers between devices, forward_layer(): gathered = lax.all_gather(mixed, 'col', axis=1, tiled=True)  104 us
    psum x2, blocking collectives, backward_layer(): lax.psum((jnp.sum(grad_before, axis=0), jnp.sum(grad_before * normed, axi...  76.5 us
    psum x2, blocking collectives, moments(): lax.psum((jnp.sum(valid), jnp.sum(valid * linear, axis=0)), 'row')  43.5 us
  transfers between devices with their start and end apart: 6, of which 6 were waited for; matrix products, arithmetic and copies ran while one was open for 4% of the time, Pallas kernels for 0%

profile of v1, /device:TPU:0, one launch (start us, length us, event | category | flops | bytes accessed | tf_op | source)
XLA Modules:
  0.0 1831.4 jit_solution(17772845330971338407)
XLA Ops:
  7.3 2.3 copy.23
  9.6 27.6 %while.10 = (s32[]{:T(128)}, f32[14,128,128]{2,1,0:T(8,128)S(1)}, s32[14,128,32]{2,1,0:T(8,128)}, s32[]{:T(128)}) while((s32[]{:T(128)}, f32[14,128,128]{2,1,0:T(8,128)S(1)}, s32[14,128,32]{2,1,0:T(8,128)}, s32[]{:T(128)}) %tuple.47), condition=%wide.region_3.4_spmd, body=%wide.region_0.3_spmd.sunk | while | flops 1634306 | bytes 247869 | solution.py:22
  11.5 0.9 convert_reduce_fusion.5
  13.5 0.9 convert_reduce_fusion.5
  15.5 0.9 convert_reduce_fusion.5
  17.4 0.9 convert_reduce_fusion.5
  19.4 0.9 convert_reduce_fusion.5
  21.4 0.9 convert_reduce_fusion.5
  23.4 0.9 convert_reduce_fusion.5
  25.3 0.9 convert_reduce_fusion.5
  27.3 0.9 convert_reduce_fusion.5
  29.3 0.9 convert_reduce_fusion.5
  31.3 0.9 convert_reduce_fusion.5
  37.2 4.7 copy.24
  41.8 1.8 gather_fusion
  43.7 5.1 add_convert_fusion.1
  49.4 54.5 %all-gather.7.cloned.1.call-done = bf16[1792,2048]{1,0:T(8,128)(2,1)} async-done(((bf16[1792,512]{1,0:T(8,128)(2,1)}), bf16[1792,2048]{1,0:T(8,128)(2,1)}) %all-gather.7.cloned.1.call-update) | async-done | bytes 7340048 | tf_op jit(solution)/shard_map/all_gather | solution.py:48
  103.9 9.5 multiply_reduce_fusion.3
  113.5 22.0 %all-reduce.2 = (f32[512]{0:T(512)S(1)}, f32[]{:T(128)}) all-reduce(f32[512]{0:T(512)S(1)} %get-tuple-element.47, f32[]{:T(128)} %convert_reduce_fusion.2), channel_id=1, replica_groups=mesh['row'=8,'col'=4] {'row'}, use_global_device_ids=true, to_apply=%region_5.6 | all-reduce | flops 513 | bytes 4104 | tf_op jit(solution)/shard_map/psum | solution.py:39
  136.2 2.6 fusion.2
  138.7 17.1 psum.68
  156.6 3.0 multiply_multiply_fusion.4
  159.6 4.5 add_convert_fusion
  164.6 49.8 %all-gather.9.cloned.1.call-done = bf16[1792,2048]{1,0:T(8,128)(2,1)} async-done(((bf16[1792,512]{1,0:T(8,128)(2,1)}), bf16[1792,2048]{1,0:T(8,128)(2,1)}) %all-gather.9.cloned.1.call-update) | async-done | bytes 7340048 | tf_op jit(solution)/shard_map/all_gather | solution.py:48
  214.4 8.9 multiply_reduce_fusion.2
  223.3 21.5 %psum.69 = f32[512]{0:T(512)S(1)} all-reduce(f32[512]{0:T(512)S(1)} %get-tuple-element.49), channel_id=1, replica_groups=mesh['row'=8,'col'=4] {'row'}, use_global_device_ids=true, to_apply=%region_11.12 | all-reduce | flops 512 | bytes 4096 | tf_op jit(solution)/shard_map/psum | solution.py:39
  245.4 2.6 fusion.3
  248.0 17.1 psum.70
  265.8 6.3 fusion.6
  272.1 19.1 %all-reduce.1 = (f32[512]{0:T(512)S(1)}, f32[512]{0:T(512)S(1)}) all-reduce(f32[512]{0:T(512)S(1)} %get-tuple-element.29, f32[512]{0:T(512)S(1)} %get-tuple-element.28), channel_id=1, replica_groups=mesh['row'=8,'col'=4] {'row'}, use_global_device_ids=true, to_apply=%region_17.18 | all-reduce | flops 1024 | bytes 8192 | tf_op jit(solution)/shard_map/psum | solution.py:63
  291.2 4.6 multiply_convert_fusion.1
  295.9 1.2 copy-done.3
  297.1 7.2 fusion.8
  304.5 1.4 copy-done.4
  305.9 9.8 fusion.11
  315.9 97.8 %reduce-scatter.3.cloned.1.call-done = f32[1792,512]{1,0:T(8,128)} async-done(((f32[1792,2048]{1,0:T(8,128)}), f32[1792,512]{1,0:T(8,128)}) %reduce-scatter.3.cloned.1.call-update) | async-done | bytes 3670032 | tf_op jit(solution)/shard_map/reduce_scatter | solution.py:83
  413.7 6.8 multiply_add_fusion.1
  420.5 3.7 fusion.5
  424.3 57.4 %all-reduce = (f32[512]{0:T(512)S(1)}, f32[512]{0:T(512)S(1)}) all-reduce(f32[512]{0:T(512)S(1)} %get-tuple-element.27, f32[512]{0:T(512)S(1)} %get-tuple-element.26), channel_id=1, replica_groups=mesh['row'=8,'col'=4] {'row'}, use_global_device_ids=true, to_apply=%region_22.23 | all-reduce | flops 1024 | bytes 8192 | tf_op jit(solution)/shard_map/psum | solution.py:63
  481.7 4.9 multiply_convert_fusion
  486.6 7.2 fusion.9
  494.2 8.8 fusion.10
  503.0 551.1 %all-gather.13.cloned.1.call-done = f32[16384,512]{1,0:T(8,128)} async-done(((f32[2048,512]{1,0:T(8,128)}), f32[16384,512]{1,0:T(8,128)}) %all-gather.13.cloned.1.call-update) | async-done | bytes 33554448 | tf_op jit(solution)/shard_map/all_gather | solution.py:76
  1054.0 17.9 reduce_sum.133
  1071.9 97.5 %reduce-scatter.5.cloned.1.call-done = f32[1792,512]{1,0:T(8,128)} async-done(((f32[1792,2048]{1,0:T(8,128)}), f32[1792,512]{1,0:T(8,128)}) %reduce-scatter.5.cloned.1.call-update) | async-done | bytes 3670032 | tf_op jit(solution)/shard_map/reduce_scatter | solution.py:83
  1169.4 8.5 multiply_add_fusion
  1177.9 631.2 %all-gather.11.cloned.1.call-done = f32[16384,512]{1,0:T(8,128)} async-done(((f32[2048,512]{1,0:T(8,128)}), f32[16384,512]{1,0:T(8,128)}) %all-gather.11.cloned.1.call-update) | async-done | bytes 33554448 | tf_op jit(solution)/shard_map/all_gather | solution.py:76
  1809.1 15.2 reduce_sum.132
  (96 shorter events, 21.3 us)
Async XLA Ops:
  7.2 207.2 %copy-start = (bf16[2048,512]{1,0:T(8,128)(2,1)S(1)}, bf16[2048,512]{1,0:T(8,128)(2,1)}, u32[]{:S(2)}) copy-start(bf16[2048,512]{1,0:T(8,128)(2,1)} %param.18) | copy-start | bytes 6291460
  7.2 96.8 %all-gather.7.cloned.1.call-start = ((), (), s32[]{:S(2)}) async-start(), calls=%async_computation.2 | async-start | bytes 9175040 | tf_op jit(solution)/shard_map/all_gather | solution.py:48
  41.8 7.0 copy-start.5
  48.8 165.6 %all-gather.9.cloned.1.call-start = ((), (), s32[]{:S(2)}) async-start(), calls=%async_computation.3 | async-start | bytes 9175040 | tf_op jit(solution)/shard_map/all_gather | solution.py:48
  113.5 43.1 %copy-start.6 = (f32[512]{0:T(512)S(1)}, f32[512]{0:T(512)}, u32[]{:S(2)}) copy-start(f32[512]{0:T(512)} %param.16) | copy-start | bytes 6148
  113.5 43.1 %copy-start.8 = (f32[512]{0:T(512)S(1)}, f32[512]{0:T(512)}, u32[]{:S(2)}) copy-start(f32[512]{0:T(512)} %param.17) | copy-start | bytes 6148
  164.1 249.6 %reduce-scatter.3.cloned.1.call-start = ((), (), s32[]{:S(2)}) async-start(), calls=%async_computation.4 | async-start | bytes 18350080 | tf_op jit(solution)/shard_map/reduce_scatter | solution.py:83
  223.3 42.5 %copy-start.7 = (f32[512]{0:T(512)S(1)}, f32[512]{0:T(512)}, u32[]{:S(2)}) copy-start(f32[512]{0:T(512)} %param.19) | copy-start | bytes 6148
  223.3 42.6 %copy-start.9 = (f32[512]{0:T(512)S(1)}, f32[512]{0:T(512)}, u32[]{:S(2)}) copy-start(f32[512]{0:T(512)} %param.20) | copy-start | bytes 6148
  291.2 4.7 copy-start.10
  291.2 4.7 copy-start.12
  295.9 1.2 copy-start.3
  304.4 1.5 copy-start.4
  304.4 749.6 %all-gather.13.cloned.1.call-start = ((), (), s32[]{:S(2)}) async-start(), calls=%async_computation.7 | async-start | bytes 37748736 | tf_op jit(solution)/shard_map/all_gather | solution.py:76
  315.6 853.8 %reduce-scatter.5.cloned.1.call-start = ((), (), s32[]{:S(2)}) async-start(), calls=%async_computation.5 | async-start | bytes 18350080 | tf_op jit(solution)/shard_map/reduce_scatter | solution.py:83
  413.7 6.8 copy-start.2
  481.7 4.9 copy-start.11
  481.7 5.0 copy-start.13
  481.7 4.9 copy-start.14
  493.9 1315.3 %all-gather.11.cloned.1.call-start = ((), (), s32[]{:S(2)}) async-start(), calls=%async_computation.6 | async-start | bytes 37748736 | tf_op jit(solution)/shard_map/all_gather | solution.py:76
  1809.1 15.2 copy-start.1
Sparse Core Ops, SparseCore 0:
  48.9 55.0 all-gather.6
  164.2 50.1 all-gather.8
  304.5 109.1 reduce-scatter.2
  415.7 638.3 all-gather.12
  1056.5 112.9 reduce-scatter.4
  1171.4 637.7 all-gather.10
